TPU v7x, 32 devices: a whole 2x2x4 slice. The times are simulated.
32 devices in a mesh: group: 2 (over x), src: 16 (over z, y, core).
Axes of the slice: x: 2, y: 2, z: 4, core: 2. Of those that a mesh axis runs over, the one named last changes fastest.
Arguments:
- rcv_points: float32 [3, 4096], P(None, ('group', 'src')), parts along dimension 1, may hold values from -1 to 1
- rcv_normals: float32 [3, 4096], P(None, ('group', 'src')), parts along dimension 1, may hold values from -4 to 4
- left_modes: float32 [8, 4096], P(None, ('group', 'src')), parts along dimension 1, may hold values from -5 to 5
- vertices: float32 [3, 2048], P(None, ('group', 'src')), parts along dimension 1, may hold values from -1 to 1
- connect: int32 [2, 4096], P(None, ('group', 'src')), parts along dimension 1, may hold values from 0 to 1023, as said below
- right_modes: float32 [8, 4096], P(None, ('group', 'src')), parts along dimension 1, may hold values from -0.125 to 0.125
- mode_weights: float32 [16], P('group'), parts along dimension 0, may hold values from 0.25 to 1
Outputs:
- rcv_grad: float32 [6, 4096], P(None, ('group', 'src')), parts along dimension 1
- vert_grad: float32 [3, 2048], P(None, ('group', 'src')), parts along dimension 1
There are 2 independent parts, one for each index of `group`. A program takes and returns all parts, laid end to end along the dimension named above; each array names one. Nothing has to cross between parts.
Inputs may be any that keep to these rules, and one draw needn't show every extreme that they name: `connect`: a panel's first vertex is one of the 64 vertices held at the same index of src as the panel, and its second vertex is the next vertex number.
All inputs are finite; a program needn't handle non-finite values.
Results may differ from a plain program's by a relative error of at most 0.0003.
Values sent between devices are 32-bit elements; how exact they have to be, the bound alone decides.
No kernel may reach another device: no remote copies, remote signals or barrier semaphores. Data moves between devices by JAX's collectives and lax.ppermute only.
A program may use at most 64 MiB of HBM per device.

v0:
```python
import math
import jax
import jax.numpy as jnp
from jax import lax
from jax.sharding import PartitionSpec as P

core_term = 0.05
inverse_four_pi = 0.25 / math.pi


def shifted(value, axis, steps):
    count = lax.axis_size(axis)
    leading, last = (max(0, -steps), min(count, count - steps))
    return lax.ppermute(value, axis, [(source, source + steps) for source in range(leading, last)])


def lift_points(raw):
    return jnp.stack([raw[0], raw[1], 0.5 + 0.2 * raw[2]])


def place_points(raw):
    return jnp.stack([raw[0], raw[1], 0.2 * raw[2]])


def tile_energy(points, normals, first_end, second_end, coefficient):
    rel_first = points[:, None, :] - first_end[:, :, None]
    rel_second = points[:, None, :] - second_end[:, :, None]
    segment = (second_end - first_end)[:, :, None]
    cross_x = rel_first[1] * rel_second[2] - rel_first[2] * rel_second[1]
    cross_y = rel_first[2] * rel_second[0] - rel_first[0] * rel_second[2]
    cross_z = rel_first[0] * rel_second[1] - rel_first[1] * rel_second[0]
    cross_sq = cross_x * cross_x + cross_y * cross_y + cross_z * cross_z
    dist_first = jnp.sqrt(jnp.sum(rel_first * rel_first, axis=0))
    dist_second = jnp.sqrt(jnp.sum(rel_second * rel_second, axis=0))
    along_term = jnp.sum(segment * (rel_first / dist_first - rel_second / dist_second), axis=0)
    span_sq = jnp.sum(segment * segment, axis=0)
    denominator = cross_sq + core_term * (span_sq + 1.0)
    normal_term = (
        normals[0][None, :] * cross_x
        + normals[1][None, :] * cross_y
        + normals[2][None, :] * cross_z
    )
    influence = inverse_four_pi * normal_term * along_term / denominator
    return jnp.sum(coefficient * influence)


def tile_gradients(points, normals, first_end, second_end, coefficient):
    return jax.grad(tile_energy, argnums=(0, 1, 2, 3))(
        points, normals, first_end, second_end, coefficient
    )


def on_device(rcv_points, rcv_normals, left_modes, vertices, connect, right_modes, mode_weights):
    own_count = vertices.shape[1]
    next_first = shifted(vertices[:, :1], "src", -1)
    extended = jnp.concatenate([vertices, next_first], axis=1)
    places = place_points(extended)
    base_vertex = lax.axis_index("src") * own_count
    local_first = connect[0] - base_vertex
    local_second = local_first + 1
    first_end = places[:, local_first]
    second_end = places[:, local_second]
    points = lift_points(rcv_points)
    chain_scale = jnp.array([1.0, 1.0, 0.2], dtype=jnp.float32)[:, None]
    weighted = right_modes * mode_weights[:, None]
    receiver_count = rcv_points.shape[1] * lax.axis_size("src")
    source_count = connect.shape[1]
    start_totals = (
        jnp.zeros((3, source_count), jnp.float32),
        jnp.zeros((3, source_count), jnp.float32),
        jnp.zeros((6, receiver_count), jnp.float32),
    )
    shard_points = lax.all_gather(points, "src", axis=1, tiled=True)
    shard_normals = lax.all_gather(rcv_normals, "src", axis=1, tiled=True)
    shard_left = lax.all_gather(left_modes, "src", axis=1, tiled=True)
    row_count = shard_points.shape[1]
    width_rows = math.gcd(row_count, 2048)

    def advance(number, inner):
        sum_first, sum_second, receiver_buffer = inner
        local_start = number * width_rows
        block_points = lax.dynamic_slice_in_dim(shard_points, local_start, width_rows, 1)
        block_normals = lax.dynamic_slice_in_dim(shard_normals, local_start, width_rows, 1)
        block_left = lax.dynamic_slice_in_dim(shard_left, local_start, width_rows, 1)
        coefficient = jnp.einsum("mj,mi->ji", weighted, block_left, precision=lax.Precision.HIGHEST)
        grads = tile_gradients(block_points, block_normals, first_end, second_end, coefficient)
        rows_out = jnp.concatenate([grads[0] * chain_scale, grads[1]], axis=0)
        receiver_buffer = lax.dynamic_update_slice_in_dim(receiver_buffer, rows_out, local_start, 1)
        return (sum_first + grads[2], sum_second + grads[3], receiver_buffer)

    sum_first, sum_second, receiver_buffer = lax.fori_loop(
        0, row_count // width_rows, advance, start_totals
    )
    rcv_grad = lax.psum_scatter(receiver_buffer, "src", scatter_dimension=1, tiled=True)
    vertex_partial = jnp.zeros((3, own_count + 1), jnp.float32)
    vertex_partial = (
        vertex_partial.at[:, local_first].add(sum_first).at[:, local_second].add(sum_second)
    )
    incoming = shifted(vertex_partial[:, own_count:], "src", 1)
    own_part = vertex_partial[:, :own_count]
    own_part = jnp.concatenate([own_part[:, :1] + incoming, own_part[:, 1:]], axis=1)
    vert_grad = own_part * chain_scale
    return (rcv_grad, vert_grad)


def solution(mesh):
    in_specs = (
        P(None, ("group", "src")),
        P(None, ("group", "src")),
        P(None, ("group", "src")),
        P(None, ("group", "src")),
        P(None, ("group", "src")),
        P(None, ("group", "src")),
        P("group"),
    )
    out_specs = (P(None, ("group", "src")), P(None, ("group", "src")))
    return jax.shard_map(
        on_device, mesh=mesh, in_specs=in_specs, out_specs=out_specs, check_vma=False
    )
```

profile of v0, /device:TPU:0, one launch (start us, length us, event | category | flops | bytes accessed | tf_op | source)
XLA Modules:
  0.0 154.4 jit_solution(849035136935577808)
XLA Ops:
  7.2 0.0 reduce-scatter.2.cloned.1.call-start
  7.2 1.3 collective-permute-start
  8.5 0.7 multiply_add_fusion.1
  9.2 0.7 slice.81
  9.9 23.8 %all_gather.10 = f32[3,2048]{1,0:T(4,128)S(1)} all-gather(f32[3,128]{1,0:T(4,128)S(1)} %pad_maximum_fusion.3), channel_id=1, replica_groups=mesh['group'=2,'src'=16] {'src'}, dimensions={1}, use_global_device_ids=true | all-gather | bytes 26112 | tf_op jit(solution)/shard_map/all_gather | solution.py:73
  33.7 17.7 %all_gather.9 = f32[3,2048]{1,0:T(4,128)S(1)} all-gather(f32[3,128]{1,0:T(4,128)} %param.9), channel_id=1, replica_groups=mesh['group'=2,'src'=16] {'src'}, dimensions={1}, use_global_device_ids=true | all-gather | bytes 26112 | tf_op jit(solution)/shard_map/all_gather | solution.py:74
  51.4 19.2 %all_gather.11 = f32[8,2048]{1,0:T(8,128)S(1)} all-gather(f32[8,128]{1,0:T(8,128)} %param.10), channel_id=1, replica_groups=mesh['group'=2,'src'=16] {'src'}, dimensions={1}, use_global_device_ids=true | all-gather | bytes 69632 | tf_op jit(solution)/shard_map/all_gather | solution.py:75
  70.6 0.7 fusion.24
  71.3 0.0 collective-permute-done
  71.3 0.8 pad_maximum_fusion.1
  72.1 0.1 copy.26
  72.2 0.6 gather_fusion.1
  72.9 0.1 copy.29
  72.9 0.7 gather_fusion
  73.6 0.1 copy.27
  73.7 0.8 fusion.15
  74.5 0.0 copy-start.2
  74.5 0.0 copy-start.3
  74.6 0.3 multiply_divide_fusion.1
  74.9 0.3 multiply_divide_fusion.2
  75.3 0.0 copy-done.2
  75.3 0.0 copy-done.3
  75.3 1.8 %divide_multiply_fusion.1 = (f32[128,2048]{1,0:T(8,128)S(1)}, f32[128,2048]{1,0:T(8,128)S(1)}, f32[128,2048]{1,0:T(8,128)S(1)}, f32[128,2048]{1,0:T(8,128)S(1)},...) fusion(f32[128]{0:T(128)S(1)} %add_multiply_fusion.2, f32[2048]{0:T(1024)S(1)} %bitcast.136, ...), kind=kOutput, calls=%fused_computation.109 | convolution fusion | flops 31196160 | bytes 13726240 | tf_op jit(solution)/shard_map/while/body/eval_jaxpr/mj,mi->ji/dot_general | solution.py:85
  77.1 2.5 %multiply_reduce_fusion = (f32[3,128]{1,0:T(4,128)S(1)}, f32[128,2048]{1,0:T(8,128)S(1)}, f32[128,2048]{1,0:T(8,128)S(1)}, f32[128,2048]{1,0:T(8,128)S(1)}) fusion(f32[128,2048]{1,0:T(8,128)S(1)} %get-tuple-element.62, f32[128,2048]{1,0:T(8,128)S(1)} %get-tuple-element.92, f32[3,128]{1,0:T(4,128)S(1)} %bitcast.127, f32[128,2048]{1,0:T(8,128)S(1)} %get-tuple-element.94, ...), kind=kLoop, calls=%fused_computation.36 | loop fusion | flops 12582528 | bytes 8419328 | tf_op jit(solution)/shard_map/while/body/eval_jaxpr/transpose(jvp())/reduce_sum | solution.py:35
  79.6 0.2 multiply_multiply_fusion.3
  79.8 0.2 multiply_multiply_fusion.1
  80.1 0.6 fusion.28
  80.6 2.0 %multiply_bitcast_fusion.5 = (f32[1,128,2048]{2,1,0:T(8,128)}, f32[128,2048]{1,0:T(8,128)}, f32[128,2048]{1,0:T(8,128)S(1)}) fusion(f32[3,128,2048]{2,1,0:T(8,128)S(1)} %get-tuple-element.95, f32[128,2048]{1,0:T(8,128)S(1)} %get-tuple-element.67, f32[128,2048]{1,0:T(8,128)S(1)} %get-tuple-element.54, f32[2048]{0:T(1024)S(1)} %broadcast_multiply_fusion.2, ...), kind=kLoop, calls=%fused_computation.57 | loop fusion | flops 2359296 | bytes 9445376 | tf_op jit(solution)/shard_map/while/body/eval_jaxpr/transpose(jvp())/broadcast_in_dim | solution.py:31
  82.6 2.2 %multiply_bitcast_fusion.3 = (f32[1,128,2048]{2,1,0:T(8,128)S(1)}, f32[128,2048]{1,0:T(8,128)}, f32[1,128,2048]{2,1,0:T(8,128)S(1)}, f32[128,2048]{1,0:T(8,128)}...) fusion(f32[3,128,2048]{2,1,0:T(8,128)S(1)} %get-tuple-element.95, f32[128,2048]{1,0:T(8,128)S(1)} %get-tuple-element.66, ...), kind=kLoop, calls=%fused_computation.55 | loop fusion | flops 5236736 | bytes 11575296 | tf_op jit(solution)/shard_map/while/body/eval_jaxpr/transpose(jvp())/broadcast_in_dim | solution.py:30
  84.9 4.8 %multiply_bitcast_fusion.11 = (f32[1,128,2048]{2,1,0:T(8,128)S(1)}, f32[1,128,2048]{2,1,0:T(8,128)S(1)}, f32[1,128,2048]{2,1,0:T(8,128)S(1)}, f32[1,128,2048]{2,...) fusion(f32[128,2048]{1,0:T(8,128)} %get-tuple-element.56, ...), kind=kLoop, calls=%fused_computation.65 | loop fusion | flops 3145728 | bytes 18874368 | tf_op jit(solution)/shard_map/while/body/eval_jaxpr/transpose(jvp())/broadcast_in_dim | solution.py:31
  89.7 3.4 %fusion.27 = (f32[3,128]{1,0:T(4,128)S(1)}, f32[3,2048]{1,0:T(4,128)S(1)}) fusion(f32[1,128,2048]{2,1,0:T(8,128)} %get-tuple-element.88, f32[1,128,2048]{2,1,0:T(8,128)S(1)} %get-tuple-element.70, f32[1,128,2048]{2,1,0:T(8,128)} %get-tuple-element.89, f32[1,128,2048]{2,1,0:T(8,128)S(1)} %get-tuple-element.58, f32[1,128,2048]{2,1,0:T(8,128)} %get-tuple-element.90, ...), kind=kLoop, calls=%fused_computation.111 | loop fusion | flops 11003520 | bytes 9490944 | tf_op jit(solution)/shard_map/while/body/eval_jaxpr/transpose(jvp())/reduce_sum | solution.py:26
  93.1 0.0 copy-done
  93.1 0.0 copy-start.1
  93.1 1.9 %fusion.26 = (f32[3,128]{1,0:T(4,128)S(1)}, f32[3,2048]{1,0:T(4,128)S(1)}) fusion(f32[1,128,2048]{2,1,0:T(8,128)S(1)} %get-tuple-element.84, f32[1,128,2048]{2,1,0:T(8,128)S(1)} %get-tuple-element.85, f32[1,128,2048]{2,1,0:T(8,128)S(1)} %get-tuple-element.86, f32[1,128,2048]{2,1,0:T(8,128)S(1)} %copy-done, f32[1,128,2048]{2,1,0:T(8,128)S(1)} %get-tuple-element.73, ...), kind=kLoop, calls=%fused_computation.110 | loop fusion | flops 11789952 | bytes 9490944 | tf_op jit(solution)/shard_map/while/body/eval_jaxpr/transpose(jvp())/reduce_sum | solution.py:27
  95.0 0.1 copy.31
  95.1 0.1 copy.30
  95.2 1.0 scatter_custom_fusion
  96.2 1.2 scatter_fusion
  97.5 0.0 copy-done.1
  97.5 0.1 add_multiply_fusion.1
  97.6 0.6 pad_maximum_fusion
  98.2 0.0 reduce-scatter.2.cloned.1.call-update
  98.3 2.2 %collective-permute-start.1 = (f32[3,1]{0,1:T(1,128)S(1)}, f32[3,1]{0,1:T(1,128)S(1)}, u32[]{:S(2)}, u32[]{:S(2)}) collective-permute-start(f32[3,1]{0,1:T(1,128)S(1)} %slice.108), channel_id=1, source_target_pairs={{0,1},{1,2},{2,3},{3,4},{4,5},{5,6},{6,7},{7,8},{8,9},{9,10},{10,1... | collective-permute-start | bytes 44 | tf_op jit(solution)/shard_map/ppermute | solution.py:14
  100.5 0.1 copy.33
  100.6 0.7 collective-permute-done.1
  101.3 0.1 copy.32
  101.4 0.7 maximum_multiply_fusion
  102.1 45.5 %reduce-scatter.2.cloned.1.call-done = f32[6,128]{1,0:T(8,128)} async-done(((f32[6,2048]{1,0:T(8,128)}), f32[6,128]{1,0:T(8,128)}) %reduce-scatter.2.cloned.1.call-update) | async-done | bytes 3088 | tf_op jit(solution)/shard_map/reduce_scatter | solution.py:94
  (17 shorter events, 0.2 us)
Async XLA Ops:
  7.2 140.4 %reduce-scatter.2.cloned.1.call-start = ((), (), s32[]{:S(2)}) async-start(), calls=%async_computation.1 | async-start | bytes 69632 | tf_op jit(solution)/shard_map/reduce_scatter | solution.py:94
  7.2 64.1 %collective-permute-start = (f32[3,1]{1,0:T(4,128)}, f32[3,1]{1,0:T(4,128)S(1)}, u32[]{:S(2)}, u32[]{:S(2)}) collective-permute-start(f32[3,1]{1,0:T(4,128)} %bitcast.141), channel_id=1, source_target_pairs={{1,0},{2,1},{3,2},{4,3},{5,4},{6,5},{7,6},{8,7},{9,8},{10,9},{11,1... | collective-permute-start | bytes 44 | tf_op jit(solution)/shard_map/ppermute | solution.py:14
  74.5 0.7 copy-start.2
  74.5 0.7 copy-start.3
  89.7 3.4 %copy-start = (f32[1,128,2048]{2,1,0:T(8,128)S(1)}, f32[1,128,2048]{2,1,0:T(8,128)}, u32[]{:S(2)}) copy-start(f32[1,128,2048]{2,1,0:T(8,128)} %get-tuple-element.87) | copy-start | bytes 3145732
  93.1 4.4 %copy-start.1 = (f32[3]{0:T(128)S(1)}, f32[3]{0:T(128)}, u32[]{:S(2)}) copy-start(f32[3]{0:T(128)} %constant.34.clone) | copy-start | bytes 40
  98.3 3.1 %collective-permute-start.1 = (f32[3,1]{0,1:T(1,128)S(1)}, f32[3,1]{0,1:T(1,128)S(1)}, u32[]{:S(2)}, u32[]{:S(2)}) collective-permute-start(f32[3,1]{0,1:T(1,128)S(1)} %slice.108), channel_id=1, source_target_pairs={{0,1},{1,2},{2,3},{3,4},{4,5},{5,6},{6,7},{7,8},{8,9},{9,10},{10,1... | collective-permute-start | bytes 44 | tf_op jit(solution)/shard_map/ppermute | solution.py:14
Sparse Core Ops, SparseCore 0:
  98.4 49.1 reduce-scatter.1
where the time goes:
time: 155 us; the launch traced here: 154 us
  blocking collectives  60.7 us (39%)
  waiting for transfers between devices  46.3 us (30%)
  other arithmetic  25.1 us (16%)
  between operations  14.3 us (9%)
  starting transfers between devices  3.57 us (2%)
  local copies, waits for them, and re-layouts  2.68 us (2%)
  matrix products  1.85 us (1%)
    reduce_scatter x1, waiting for transfers between devices, on_device(): lax.psum_scatter(receiver_buffer, 'src', scatter_dimension=1, tiled=True)  45.5 us
    all_gather x1, blocking collectives, on_device(): shard_points = lax.all_gather(points, 'src', axis=1, tiled=True)  23.8 us
    all_gather x1, blocking collectives, on_device(): shard_left = lax.all_gather(left_modes, 'src', axis=1, tiled=True)  19.2 us
    all_gather x1, blocking collectives, on_device(): shard_normals = lax.all_gather(rcv_normals, 'src', axis=1, tiled=True)  17.7 us
    broadcast_in_dim x2, other arithmetic, tile_energy(): cross_z = rel_first[0] * rel_second[1] - rel_first[1] * rel_second[0]  6.79 us
    ppermute x2, starting transfers between devices, shifted(): lax.ppermute(value, axis, [(source, source + steps) for source in range(l...  3.54 us
    reduce_sum x1, other arithmetic, tile_energy(): rel_first = points[:, None, :] - first_end[:, :, None]  3.41 us
  transfers between devices with their start and end apart: 3, of which 2 were waited for; matrix products, arithmetic and copies ran while one was open for 2% of the time, Pallas kernels for 0%

commit v1 on v0

--- a/solution.py
+++ b/solution.py
@@ -51,6 +51,16 @@
 
 
 def on_device(rcv_points, rcv_normals, left_modes, vertices, connect, right_modes, mode_weights):
+
+    def raise_the_quotas(row_data, u_in):
+        return jnp.split(
+            jax.lax.all_gather(
+                jnp.concatenate([row_data, u_in], 0), axis_name="src", axis=1, tiled=True
+            ),
+            [row_data.shape[0]],
+            0,
+        )
+
     own_count = vertices.shape[1]
     next_first = shifted(vertices[:, :1], "src", -1)
     extended = jnp.concatenate([vertices, next_first], axis=1)
@@ -70,8 +80,7 @@
         jnp.zeros((3, source_count), jnp.float32),
         jnp.zeros((6, receiver_count), jnp.float32),
     )
-    shard_points = lax.all_gather(points, "src", axis=1, tiled=True)
-    shard_normals = lax.all_gather(rcv_normals, "src", axis=1, tiled=True)
+    shard_points, shard_normals = raise_the_quotas(points, rcv_normals)
     shard_left = lax.all_gather(left_modes, "src", axis=1, tiled=True)
     row_count = shard_points.shape[1]
     width_rows = math.gcd(row_count, 2048)

time: 155 us -> 138 us (0.89)
  blocking collectives: 60.7 us -> 41.8 us
    all_gather x2 -> x1, blocking collectives: 41.5 us -> 23.9 us  [raise_the_quotas(): jax.lax.all_gather(jnp.concatenate([row_data, u_in], 0), axis_name='src',...]
  transfers between devices with their start and end apart: 3 -> 3, of which waited for: 2 -> 2; matrix products, arithmetic and copies ran while one was open for 2% -> 3% of each run, Pallas kernels for 0% -> 0%
where the time goes in v1:
time: 138 us; the launch traced here: 137 us
  waiting for transfers between devices  47.3 us (34%)
  blocking collectives  41.8 us (30%)
  other arithmetic  25.8 us (19%)
  between operations  14.3 us (10%)
  starting transfers between devices  3.57 us (3%)
  local copies, waits for them, and re-layouts  2.69 us (2%)
  matrix products  1.86 us (1%)
    reduce_scatter x1, waiting for transfers between devices, on_device(): lax.psum_scatter(receiver_buffer, 'src', scatter_dimension=1, tiled=True)  46.5 us
    all_gather x1, blocking collectives, raise_the_quotas(): jax.lax.all_gather(jnp.concatenate([row_data, u_in], 0), axis_name='src',...  23.9 us
    all_gather x1, blocking collectives, on_device(): shard_left = lax.all_gather(left_modes, 'src', axis=1, tiled=True)  17.9 us
    broadcast_in_dim x2, other arithmetic, tile_energy(): cross_z = rel_first[0] * rel_second[1] - rel_first[1] * rel_second[0]  6.79 us
    ppermute x2, starting transfers between devices, shifted(): lax.ppermute(value, axis, [(source, source + steps) for source in range(l...  3.54 us
    reduce_sum x1, other arithmetic, tile_energy(): rel_first = points[:, None, :] - first_end[:, :, None]  3.41 us
  transfers between devices with their start and end apart: 3, of which 2 were waited for; matrix products, arithmetic and copies ran while one was open for 3% of the time, Pallas kernels for 0%

profile of v1, /device:TPU:0, one launch (start us, length us, event | category | flops | bytes accessed | tf_op | source)
XLA Modules:
  0.0 137.2 jit_solution(15015483532067476208)
XLA Ops:
  7.2 0.0 reduce-scatter.2.cloned.1.call-start
  7.2 1.3 collective-permute-start
  8.5 0.7 multiply_add_fusion.1
  9.2 0.7 slice.83
  9.9 0.7 pad_maximum_fusion.1
  10.6 23.9 %all_gather.6 = f32[6,2048]{1,0:T(8,128)S(1)} all-gather(f32[6,128]{1,0:T(8,128)S(1)} %pad_maximum_fusion.1), channel_id=1, replica_groups=mesh['group'=2,'src'=16] {'src'}, dimensions={1}, use_global_device_ids=true | all-gather | bytes 52224 | tf_op jit(solution)/shard_map/all_gather | solution.py:57
  34.5 17.9 %all_gather.7 = f32[8,2048]{1,0:T(8,128)S(1)} all-gather(f32[8,128]{1,0:T(8,128)} %param.10), channel_id=1, replica_groups=mesh['group'=2,'src'=16] {'src'}, dimensions={1}, use_global_device_ids=true | all-gather | bytes 69632 | tf_op jit(solution)/shard_map/all_gather | solution.py:84
  52.4 0.7 fusion.24
  53.1 0.0 collective-permute-done
  53.1 0.8 pad_maximum_fusion.2
  53.9 0.1 copy.26
  54.0 0.6 gather_fusion.1
  54.6 0.1 copy.29
  54.7 0.7 gather_fusion
  55.4 0.1 copy.27
  55.5 0.8 fusion.15
  56.3 0.0 copy-start.2
  56.3 0.0 copy-start.3
  56.3 0.3 multiply_divide_fusion.1
  56.7 0.3 multiply_divide_fusion.2
  57.0 0.0 copy-done.2
  57.0 0.0 copy-done.3
  57.1 1.9 %divide_multiply_fusion.1 = (f32[128,2048]{1,0:T(8,128)S(1)}, f32[128,2048]{1,0:T(8,128)S(1)}, f32[128,2048]{1,0:T(8,128)S(1)}, f32[128,2048]{1,0:T(8,128)S(1)},...) fusion(f32[128]{0:T(128)S(1)} %add_multiply_fusion.2, f32[2048]{0:T(1024)S(1)} %bitcast.136, ...), kind=kOutput, calls=%fused_computation.109 | convolution fusion | flops 31196160 | bytes 13726240 | tf_op jit(solution)/shard_map/while/body/eval_jaxpr/mj,mi->ji/dot_general | solution.py:94
  58.9 2.5 %multiply_reduce_fusion = (f32[3,128]{1,0:T(4,128)S(1)}, f32[128,2048]{1,0:T(8,128)S(1)}, f32[128,2048]{1,0:T(8,128)S(1)}, f32[128,2048]{1,0:T(8,128)S(1)}) fusion(f32[128,2048]{1,0:T(8,128)S(1)} %get-tuple-element.62, f32[128,2048]{1,0:T(8,128)S(1)} %get-tuple-element.92, f32[3,128]{1,0:T(4,128)S(1)} %bitcast.127, f32[128,2048]{1,0:T(8,128)S(1)} %get-tuple-element.94, ...), kind=kLoop, calls=%fused_computation.36 | loop fusion | flops 12582528 | bytes 8419328 | tf_op jit(solution)/shard_map/while/body/eval_jaxpr/transpose(jvp())/reduce_sum | solution.py:35
  61.4 0.2 multiply_multiply_fusion.3
  61.6 0.2 multiply_multiply_fusion.1
  61.8 0.6 fusion.28
  62.4 2.0 %multiply_bitcast_fusion.5 = (f32[1,128,2048]{2,1,0:T(8,128)}, f32[128,2048]{1,0:T(8,128)}, f32[128,2048]{1,0:T(8,128)S(1)}) fusion(f32[3,128,2048]{2,1,0:T(8,128)S(1)} %get-tuple-element.98, f32[128,2048]{1,0:T(8,128)S(1)} %get-tuple-element.67, f32[128,2048]{1,0:T(8,128)S(1)} %get-tuple-element.54, f32[2048]{0:T(1024)S(1)} %broadcast_multiply_fusion.2, ...), kind=kLoop, calls=%fused_computation.57 | loop fusion | flops 2359296 | bytes 9445376 | tf_op jit(solution)/shard_map/while/body/eval_jaxpr/transpose(jvp())/broadcast_in_dim | solution.py:31
  64.4 2.2 %multiply_bitcast_fusion.3 = (f32[1,128,2048]{2,1,0:T(8,128)S(1)}, f32[128,2048]{1,0:T(8,128)}, f32[1,128,2048]{2,1,0:T(8,128)S(1)}, f32[128,2048]{1,0:T(8,128)}...) fusion(f32[3,128,2048]{2,1,0:T(8,128)S(1)} %get-tuple-element.98, f32[128,2048]{1,0:T(8,128)S(1)} %get-tuple-element.66, ...), kind=kLoop, calls=%fused_computation.55 | loop fusion | flops 5236736 | bytes 11575296 | tf_op jit(solution)/shard_map/while/body/eval_jaxpr/transpose(jvp())/broadcast_in_dim | solution.py:30
  66.7 4.8 %multiply_bitcast_fusion.11 = (f32[1,128,2048]{2,1,0:T(8,128)S(1)}, f32[1,128,2048]{2,1,0:T(8,128)S(1)}, f32[1,128,2048]{2,1,0:T(8,128)S(1)}, f32[1,128,2048]{2,...) fusion(f32[128,2048]{1,0:T(8,128)} %get-tuple-element.56, ...), kind=kLoop, calls=%fused_computation.65 | loop fusion | flops 3145728 | bytes 18874368 | tf_op jit(solution)/shard_map/while/body/eval_jaxpr/transpose(jvp())/broadcast_in_dim | solution.py:31
  71.5 3.4 %fusion.27 = (f32[3,128]{1,0:T(4,128)S(1)}, f32[3,2048]{1,0:T(4,128)S(1)}) fusion(f32[1,128,2048]{2,1,0:T(8,128)} %get-tuple-element.88, f32[1,128,2048]{2,1,0:T(8,128)S(1)} %get-tuple-element.70, f32[1,128,2048]{2,1,0:T(8,128)} %get-tuple-element.89, f32[1,128,2048]{2,1,0:T(8,128)S(1)} %get-tuple-element.58, f32[1,128,2048]{2,1,0:T(8,128)} %get-tuple-element.90, ...), kind=kLoop, calls=%fused_computation.111 | loop fusion | flops 11003520 | bytes 9490944 | tf_op jit(solution)/shard_map/while/body/eval_jaxpr/transpose(jvp())/reduce_sum | solution.py:26
  74.9 0.0 copy-done
  74.9 0.0 copy-start.1
  74.9 1.9 %fusion.26 = (f32[3,128]{1,0:T(4,128)S(1)}, f32[3,2048]{1,0:T(4,128)S(1)}) fusion(f32[1,128,2048]{2,1,0:T(8,128)S(1)} %get-tuple-element.84, f32[1,128,2048]{2,1,0:T(8,128)S(1)} %get-tuple-element.85, f32[1,128,2048]{2,1,0:T(8,128)S(1)} %get-tuple-element.86, f32[1,128,2048]{2,1,0:T(8,128)S(1)} %copy-done, f32[1,128,2048]{2,1,0:T(8,128)S(1)} %get-tuple-element.73, ...), kind=kLoop, calls=%fused_computation.110 | loop fusion | flops 11789952 | bytes 9490944 | tf_op jit(solution)/shard_map/while/body/eval_jaxpr/transpose(jvp())/reduce_sum | solution.py:27
  76.8 0.1 copy.31
  76.9 0.1 copy.30
  77.0 1.0 scatter_custom_fusion
  78.0 1.2 scatter_fusion
  79.3 0.0 copy-done.1
  79.3 0.1 add_multiply_fusion.1
  79.4 0.6 pad_maximum_fusion
  80.0 0.0 reduce-scatter.2.cloned.1.call-update
  80.1 2.2 %collective-permute-start.1 = (f32[3,1]{0,1:T(1,128)S(1)}, f32[3,1]{0,1:T(1,128)S(1)}, u32[]{:S(2)}, u32[]{:S(2)}) collective-permute-start(f32[3,1]{0,1:T(1,128)S(1)} %slice.111), channel_id=1, source_target_pairs={{0,1},{1,2},{2,3},{3,4},{4,5},{5,6},{6,7},{7,8},{8,9},{9,10},{10,1... | collective-permute-start | bytes 44 | tf_op jit(solution)/shard_map/ppermute | solution.py:14
  82.3 0.1 copy.33
  82.4 0.7 collective-permute-done.1
  83.1 0.1 copy.32
  83.2 0.7 maximum_multiply_fusion
  83.9 46.5 %reduce-scatter.2.cloned.1.call-done = f32[6,128]{1,0:T(8,128)} async-done(((f32[6,2048]{1,0:T(8,128)}), f32[6,128]{1,0:T(8,128)}) %reduce-scatter.2.cloned.1.call-update) | async-done | bytes 3088 | tf_op jit(solution)/shard_map/reduce_scatter | solution.py:103
  (17 shorter events, 0.2 us)
Async XLA Ops:
  7.2 123.2 %reduce-scatter.2.cloned.1.call-start = ((), (), s32[]{:S(2)}) async-start(), calls=%async_computation.1 | async-start | bytes 69632 | tf_op jit(solution)/shard_map/reduce_scatter | solution.py:103
  7.2 45.9 %collective-permute-start = (f32[3,1]{1,0:T(4,128)}, f32[3,1]{1,0:T(4,128)S(1)}, u32[]{:S(2)}, u32[]{:S(2)}) collective-permute-start(f32[3,1]{1,0:T(4,128)} %bitcast.141), channel_id=1, source_target_pairs={{1,0},{2,1},{3,2},{4,3},{5,4},{6,5},{7,6},{8,7},{9,8},{10,9},{11,1... | collective-permute-start | bytes 44 | tf_op jit(solution)/shard_map/ppermute | solution.py:14
  56.3 0.7 copy-start.2
  56.3 0.7 copy-start.3
  71.5 3.4 %copy-start = (f32[1,128,2048]{2,1,0:T(8,128)S(1)}, f32[1,128,2048]{2,1,0:T(8,128)}, u32[]{:S(2)}) copy-start(f32[1,128,2048]{2,1,0:T(8,128)} %get-tuple-element.87) | copy-start | bytes 3145732
  74.9 4.4 %copy-start.1 = (f32[3]{0:T(128)S(1)}, f32[3]{0:T(128)}, u32[]{:S(2)}) copy-start(f32[3]{0:T(128)} %constant.34.clone) | copy-start | bytes 40
  80.1 3.1 %collective-permute-start.1 = (f32[3,1]{0,1:T(1,128)S(1)}, f32[3,1]{0,1:T(1,128)S(1)}, u32[]{:S(2)}, u32[]{:S(2)}) collective-permute-start(f32[3,1]{0,1:T(1,128)S(1)} %slice.111), channel_id=1, source_target_pairs={{0,1},{1,2},{2,3},{3,4},{4,5},{5,6},{6,7},{7,8},{8,9},{9,10},{10,1... | collective-permute-start | bytes 44 | tf_op jit(solution)/shard_map/ppermute | solution.py:14
Sparse Core Ops, SparseCore 0:
  80.2 50.1 reduce-scatter.1
